TPU v7x, 256 devices: a whole 4x4x8 slice. The times are simulated.
256 devices in a mesh: samp: 16 (over z_hi, x, core), gene: 4 (over z_lo), snp: 4 (over y).
Axes of the slice: x: 4, y: 4, z: 8 (z_hi: 2, z_lo: 4; z = z_hi * 4 + z_lo), core: 2. Of those that a mesh axis runs over, the one named last changes fastest.
Arguments:
- expression: bfloat16 [4096, 16384], P('samp', ('gene', 'snp')), may hold values from -6 to 6
- loadings: bfloat16 [16384, 128], P(('gene', 'snp')), may hold values from -0.046875 to 0.046875
- dosage: bfloat16 [4096, 16384], P(None, ('gene', 'snp')), may hold values from 0 to 2
Outputs:
- assoc: bfloat16 [16, 16, 64, 16384], P(None, 'samp', None, ('gene', 'snp'))
All inputs are finite; a program needn't handle non-finite values.
Results may differ from a plain program's by a relative error of at most 0.0065.
Values may be sent and summed in bfloat16 or wider, within the bound.
No kernel may reach another device: no remote copies, remote signals or barrier semaphores. Data moves between devices by JAX's collectives and lax.ppermute only.
A program may use at most 64 MiB of HBM per device.

v0:
```python
import jax
import jax.numpy as jnp
from jax import lax
from jax.sharding import PartitionSpec as P

ridge_factor = 1.0
ridge_sample = 1.0


def body(expression, loadings, dosage):
    contract = (((0,), (0,)), ((), ()))
    factor_count = loadings.shape[1]
    identity = jnp.eye(factor_count, dtype=jnp.float32)
    panel_genes = expression.shape[1] // lax.axis_size("samp")
    all_samples = dosage.shape[0]
    snp_count = dosage.shape[1]
    block_count = lax.axis_size("gene") * lax.axis_size("snp")
    norm_scale = 1.0 / jnp.sqrt(jnp.float32(all_samples))
    local_factor = jnp.dot(expression, loadings, preferred_element_type=jnp.float32)
    local_gram = lax.dot_general(loadings, loadings, contract, preferred_element_type=jnp.float32)
    factor_sum, gram_sum = lax.psum((local_factor, local_gram), ("gene", "snp"))
    lower_gram = jnp.linalg.cholesky(gram_sum + ridge_factor * identity)
    factors = jax.scipy.linalg.cho_solve((lower_gram, True), factor_sum.T).T.astype(jnp.bfloat16)
    local_hess = lax.dot_general(factors, factors, contract, preferred_element_type=jnp.float32)
    local_cross = lax.dot_general(factors, expression, contract, preferred_element_type=jnp.float32)
    hess_sum, cross_sum = lax.psum((local_hess, local_cross), "samp")
    lower_hess = jnp.linalg.cholesky(hess_sum + ridge_sample * identity)
    fit_coef = jax.scipy.linalg.cho_solve((lower_hess, True), cross_sum).astype(jnp.bfloat16)
    fitted = lax.dot_general(
        fit_coef, factors, (((0,), (1,)), ((), ())), preferred_element_type=jnp.float32
    )
    residual_t = (expression.T.astype(jnp.float32) - fitted).astype(jnp.bfloat16)
    panel_resid = lax.all_to_all(residual_t, "samp", split_axis=0, concat_axis=1, tiled=True)
    totals = (
        jnp.dot(
            lax.all_gather(panel_resid, ("gene", "snp"), axis=0, tiled=True),
            dosage,
            preferred_element_type=jnp.float32,
        )
        * norm_scale
    )
    return totals.astype(jnp.bfloat16).reshape(block_count, 1, panel_genes, snp_count)


def solution(mesh):
    placed = (P("samp", ("gene", "snp")), P(("gene", "snp"), None), P(None, ("gene", "snp")))
    return jax.shard_map(
        body,
        mesh=mesh,
        in_specs=placed,
        out_specs=P(None, "samp", None, ("gene", "snp")),
        check_vma=False,
    )
```

profile of v0, /device:TPU:1, one launch (start us, length us, event | category | flops | bytes accessed | tf_op | source)
XLA Modules:
  0.0 548.4 jit_solution(741673774838986686)
XLA Ops:
  6.5 0.9 copy-done
  7.5 0.9 fusion.13
  8.4 2.0 fusion.14
  10.4 148.5 %all-reduce.5.cloned.1.call-done = (f32[256,128]{1,0:T(8,128)}, f32[128,128]{0,1:T(8,128)}) async-done(((f32[256,128]{1,0:T(8,128)}, f32[128,128]{0,1:T(8,128)}), (f32[256,128]{1,0:T(8,128)}, f32[128,128]{0,1:T(8,128)})) %all-reduce.5.cloned.1.call-update) | async-done | bytes 196624 | tf_op jit(solution)/shard_map/psum | solution.py:21
  159.0 0.9 convert_add_fusion.1
  159.8 0.1 copy.19
  159.9 0.9 fusion.10
  160.8 11.7 %cholesky.44 = f32[128,128]{1,0:T(8,128)S(1)} custom-call(f32[128,128]{1,0:T(8,128)S(1)} %fusion.10), custom_call_target="Cholesky" | custom-call | tf_op jit(solution)/shard_map/jit(cholesky)/cholesky | solution.py:22
  172.5 0.6 compare_reduce_fusion.1
  173.2 0.7 fusion.1
  173.8 9.8 %custom-call.16 = f32[1,128,128]{1,2,0:T(8,128)S(1)} custom-call(f32[1,128,128]{2,1,0:T(8,128)S(1)} %fusion.1), custom_call_target="InvertDiagBlocksLowerTriangular" | custom-call | tf_op jit(solution)/shard_map/jit(_cho_solve)/triangular_solve | solution.py:23
  183.6 1.2 fusion.8
  184.9 0.4 convolution_convert_fusion.1
  185.3 0.8 fusion.15
  186.1 2.1 fusion.16
  188.2 0.2 all-gather.2.cloned.1.call-start
  188.4 1.2 copy.17
  189.7 183.0 %all-reduce.7.cloned.1.call-done = (f32[128,1024]{1,0:T(8,128)}, f32[128,128]{0,1:T(8,128)}) async-done(((f32[128,1024]{1,0:T(8,128)}, f32[128,128]{0,1:T(8,128)}), (f32[128,1024]{1,0:T(8,128)}, f32[128,128]{0,1:T(8,128)})) %all-reduce.7.cloned.1.call-update) | async-done | bytes 589840 | tf_op jit(solution)/shard_map/psum | solution.py:26
  372.7 0.9 convert_add_fusion
  373.5 0.1 copy.21
  373.6 0.9 fusion.6
  374.5 11.7 %cholesky.55 = f32[128,128]{1,0:T(8,128)S(1)} custom-call(f32[128,128]{1,0:T(8,128)S(1)} %fusion.6), custom_call_target="Cholesky" | custom-call | tf_op jit(solution)/shard_map/jit(cholesky)/cholesky | solution.py:27
  386.3 0.6 compare_reduce_fusion
  386.9 0.7 fusion.2
  387.6 9.8 %custom-call.17 = f32[1,128,128]{1,2,0:T(8,128)S(1)} custom-call(f32[1,128,128]{2,1,0:T(8,128)S(1)} %fusion.2), custom_call_target="InvertDiagBlocksLowerTriangular" | custom-call | tf_op jit(solution)/shard_map/jit(_cho_solve)/triangular_solve | solution.py:28
  397.4 1.7 fusion.4
  399.0 0.6 convolution_convert_fusion
  399.6 0.3 fusion
  400.0 21.6 %all_to_all.19 = bf16[16,64,256]{2,1,0:T(8,128)(2,1)S(1)} all-to-all(bf16[16,64,256]{2,1,0:T(8,128)(2,1)S(1)} %bitcast.48), channel_id=1, replica_groups=mesh['samp'=16,'gene'=4,'snp'=4] {'samp'}, dimensions={0} | all-to-all | bytes 1048576 | tf_op jit(solution)/shard_map/all_to_all | solution.py:33
  421.6 0.8 copy.26
  422.5 104.8 %all-gather.2.cloned.1.call-done = bf16[1024,4096]{1,0:T(8,128)(2,1)} async-done(((bf16[64,4096]{1,0:T(8,128)(2,1)}), bf16[1024,4096]{1,0:T(8,128)(2,1)}) %all-gather.2.cloned.1.call-update) | async-done | bytes 8388624 | tf_op jit(solution)/shard_map/all_gather | solution.py:36
  527.3 14.6 %multiply_convert_fusion = bf16[1024,1024]{1,0:T(8,128)(2,1)} fusion(bf16[1024,4096]{1,0:T(8,128)(2,1)} %all-gather.2.cloned.1.call-done, bf16[4096,1024]{1,0:T(8,128)(2,1)} %param.6), kind=kOutput, calls=%fused_computation | convolution fusion | flops 8592031744 | bytes 18874368 | tf_op jit(solution)/shard_map/dot_general | solution.py:35
  (8 shorter events, 0.2 us)
Async XLA Ops:
  6.5 1.0 copy-start
  6.5 152.4 %all-reduce.5.cloned.1.call-start = ((), (), s32[]{:S(2)}) async-start(), calls=%async_computation.2 | async-start | bytes 393216 | tf_op jit(solution)/shard_map/psum | solution.py:21
  10.4 362.3 %all-reduce.7.cloned.1.call-start = ((), (), s32[]{:S(2)}) async-start(), calls=%async_computation.3 | async-start | bytes 1179648 | tf_op jit(solution)/shard_map/psum | solution.py:26
  188.2 339.1 %all-gather.2.cloned.1.call-start = ((), (), s32[]{:S(2)}) async-start(), calls=%async_computation.1 | async-start | bytes 8912896 | tf_op jit(solution)/shard_map/all_gather | solution.py:36
Sparse Core Ops, SparseCore 0:
  10.5 148.4 all-reduce.4
  188.3 184.3 all-reduce.6
  422.6 104.6 all-gather.1
where the time goes:
time: 549 us; the launch traced here: 548 us
  waiting for transfers between devices  436 us (79%)
  other arithmetic  49.1 us (9%)
  matrix products  24.6 us (4%)
  blocking collectives  21.6 us (4%)
  between operations  13.2 us (2%)
    psum x1, waiting for transfers between devices, body(): hess_sum, cross_sum = lax.psum((local_hess, local_cross), 'samp')  183 us
    psum x1, waiting for transfers between devices, body(): factor_sum, gram_sum = lax.psum((local_factor, local_gram), ('gene', 'snp'))  149 us
    all_gather x1, waiting for transfers between devices, body(): lax.all_gather(panel_resid, ('gene', 'snp'), axis=0, tiled=True)  105 us
    all_to_all x1, blocking collectives, body(): lax.all_to_all(residual_t, 'samp', split_axis=0, concat_axis=1, tiled=True)  21.6 us
    dot_general x1, matrix products, body(): jnp.dot(lax.all_gather(panel_resid, ('gene', 'snp'), axis=0, tiled=True),...  14.6 us
    another operation x3, other arithmetic, body(): lower_hess = jnp.linalg.cholesky(hess_sum + ridge_sample * identity)  12.4 us
    another operation x3, other arithmetic, body(): lower_gram = jnp.linalg.cholesky(gram_sum + ridge_factor * identity)  12.4 us
  transfers between devices with their start and end apart: 3, of which 3 were waited for; matrix products, arithmetic and copies ran while one was open for 0% of the time, Pallas kernels for 0%

commit v1 on v0

--- a/solution.py
+++ b/solution.py
@@ -18,7 +18,7 @@
     norm_scale = 1.0 / jnp.sqrt(jnp.float32(all_samples))
     local_factor = jnp.dot(expression, loadings, preferred_element_type=jnp.float32)
     local_gram = lax.dot_general(loadings, loadings, contract, preferred_element_type=jnp.float32)
-    factor_sum, gram_sum = lax.psum((local_factor, local_gram), ("gene", "snp"))
+    factor_sum, gram_sum = lax.psum(lax.psum((local_factor, local_gram), "gene"), "snp")
     lower_gram = jnp.linalg.cholesky(gram_sum + ridge_factor * identity)
     factors = jax.scipy.linalg.cho_solve((lower_gram, True), factor_sum.T).T.astype(jnp.bfloat16)
     local_hess = lax.dot_general(factors, factors, contract, preferred_element_type=jnp.float32)

time: 549 us -> 493 us (0.90)
  waiting for transfers between devices: 436 us -> 380 us
    psum x1 -> x2, waiting for transfers between devices: 149 us -> 98.8 us  [the longest x1 50.9 us: body(): lax.psum((local_factor, local_gram), 'gene')]
    psum x1, waiting for transfers between devices: 183 us -> 177 us  [body(): hess_sum, cross_sum = lax.psum((local_hess, local_cross), 'samp')]
  transfers between devices with their start and end apart: 3 -> 4, of which waited for: 3 -> 4; matrix products, arithmetic and copies ran while one was open for 0% -> 0% of each run, Pallas kernels for 0% -> 0%
where the time goes in v1:
time: 493 us
  waiting for transfers between devices  380 us (77%)
  other arithmetic  49.1 us (10%)
  matrix products  24.6 us (5%)
  blocking collectives  21.6 us (4%)
  between operations  13.2 us (3%)
    psum x1, waiting for transfers between devices, body(): hess_sum, cross_sum = lax.psum((local_hess, local_cross), 'samp')  177 us
    all_gather x1, waiting for transfers between devices, body(): lax.all_gather(panel_resid, ('gene', 'snp'), axis=0, tiled=True)  105 us
    psum x1, waiting for transfers between devices, body(): lax.psum((local_factor, local_gram), 'gene')  50.9 us
    psum x1, waiting for transfers between devices, body(): lax.psum(lax.psum((local_factor, local_gram), 'gene'), 'snp')  47.8 us
    all_to_all x1, blocking collectives, body(): lax.all_to_all(residual_t, 'samp', split_axis=0, concat_axis=1, tiled=True)  21.6 us
    dot_general x1, matrix products, body(): jnp.dot(lax.all_gather(panel_resid, ('gene', 'snp'), axis=0, tiled=True),...  14.6 us
    another operation x3, other arithmetic, body(): lower_gram = jnp.linalg.cholesky(gram_sum + ridge_factor * identity)  12.4 us
    another operation x3, other arithmetic, body(): lower_hess = jnp.linalg.cholesky(hess_sum + ridge_sample * identity)  12.4 us
  transfers between devices with their start and end apart: 4, of which 4 were waited for; matrix products, arithmetic and copies ran while one was open for 0% of the time, Pallas kernels for 0%

profile of v1, /device:TPU:1, one launch (start us, length us, event | category | flops | bytes accessed | tf_op | source)
XLA Modules:
  0.0 492.6 jit_solution(10428386252305050897)
XLA Ops:
  6.5 0.9 copy-done
  7.5 0.9 fusion.13
  8.4 2.0 fusion.14
  10.4 50.9 %all-reduce.11.cloned.1.call-done = (f32[256,128]{1,0:T(8,128)}, f32[128,128]{0,1:T(8,128)}) async-done(((f32[256,128]{1,0:T(8,128)}, f32[128,128]{0,1:T(8,128)}), (f32[256,128]{1,0:T(8,128)}, f32[128,128]{0,1:T(8,128)})) %all-reduce.11.cloned.1.call-update) | async-done | bytes 196624 | tf_op jit(solution)/shard_map/psum | solution.py:21
  61.4 47.8 %all-reduce.9.cloned.1.call-done = (f32[256,128]{1,0:T(8,128)}, f32[128,128]{0,1:T(8,128)}) async-done(((f32[256,128]{1,0:T(8,128)}, f32[128,128]{0,1:T(8,128)}), (f32[256,128]{1,0:T(8,128)}, f32[128,128]{0,1:T(8,128)})) %all-reduce.9.cloned.1.call-update) | async-done | bytes 196624 | tf_op jit(solution)/shard_map/psum | solution.py:21
  109.3 0.9 convert_add_fusion.1
  110.1 0.1 copy.19
  110.2 0.9 fusion.10
  111.1 11.7 %cholesky.44 = f32[128,128]{1,0:T(8,128)S(1)} custom-call(f32[128,128]{1,0:T(8,128)S(1)} %fusion.10), custom_call_target="Cholesky" | custom-call | tf_op jit(solution)/shard_map/jit(cholesky)/cholesky | solution.py:22
  122.8 0.6 compare_reduce_fusion.1
  123.5 0.7 fusion.1
  124.1 9.8 %custom-call.16 = f32[1,128,128]{1,2,0:T(8,128)S(1)} custom-call(f32[1,128,128]{2,1,0:T(8,128)S(1)} %fusion.1), custom_call_target="InvertDiagBlocksLowerTriangular" | custom-call | tf_op jit(solution)/shard_map/jit(_cho_solve)/triangular_solve | solution.py:23
  133.9 1.2 fusion.8
  135.2 0.4 convolution_convert_fusion.1
  135.6 0.8 fusion.15
  136.4 2.1 fusion.16
  138.5 0.2 all-gather.2.cloned.1.call-start
  138.7 1.2 copy.17
  140.0 176.9 %all-reduce.7.cloned.1.call-done = (f32[128,1024]{1,0:T(8,128)}, f32[128,128]{0,1:T(8,128)}) async-done(((f32[128,1024]{1,0:T(8,128)}, f32[128,128]{0,1:T(8,128)}), (f32[128,1024]{1,0:T(8,128)}, f32[128,128]{0,1:T(8,128)})) %all-reduce.7.cloned.1.call-update) | async-done | bytes 589840 | tf_op jit(solution)/shard_map/psum | solution.py:26
  316.9 0.9 convert_add_fusion
  317.8 0.9 fusion.6
  318.7 11.7 %cholesky.55 = f32[128,128]{1,0:T(8,128)S(1)} custom-call(f32[128,128]{1,0:T(8,128)S(1)} %fusion.6), custom_call_target="Cholesky" | custom-call | tf_op jit(solution)/shard_map/jit(cholesky)/cholesky | solution.py:27
  330.4 0.6 compare_reduce_fusion
  331.1 0.7 fusion.2
  331.7 9.8 %custom-call.17 = f32[1,128,128]{1,2,0:T(8,128)S(1)} custom-call(f32[1,128,128]{2,1,0:T(8,128)S(1)} %fusion.2), custom_call_target="InvertDiagBlocksLowerTriangular" | custom-call | tf_op jit(solution)/shard_map/jit(_cho_solve)/triangular_solve | solution.py:28
  341.5 1.7 fusion.4
  343.2 0.6 convolution_convert_fusion
  343.8 0.3 fusion
  344.1 21.6 %all_to_all.19 = bf16[16,64,256]{2,1,0:T(8,128)(2,1)S(1)} all-to-all(bf16[16,64,256]{2,1,0:T(8,128)(2,1)S(1)} %bitcast.48), channel_id=1, replica_groups=mesh['samp'=16,'gene'=4,'snp'=4] {'samp'}, dimensions={0} | all-to-all | bytes 1048576 | tf_op jit(solution)/shard_map/all_to_all | solution.py:33
  365.8 0.8 copy.26
  366.6 104.8 %all-gather.2.cloned.1.call-done = bf16[1024,4096]{1,0:T(8,128)(2,1)} async-done(((bf16[64,4096]{1,0:T(8,128)(2,1)}), bf16[1024,4096]{1,0:T(8,128)(2,1)}) %all-gather.2.cloned.1.call-update) | async-done | bytes 8388624 | tf_op jit(solution)/shard_map/all_gather | solution.py:36
  471.4 14.6 %multiply_convert_fusion = bf16[1024,1024]{1,0:T(8,128)(2,1)} fusion(bf16[1024,4096]{1,0:T(8,128)(2,1)} %all-gather.2.cloned.1.call-done, bf16[4096,1024]{1,0:T(8,128)(2,1)} %param.6), kind=kOutput, calls=%fused_computation | convolution fusion | flops 8592031744 | bytes 18874368 | tf_op jit(solution)/shard_map/dot_general | solution.py:35
  (11 shorter events, 0.3 us)
Async XLA Ops:
  6.5 1.0 copy-start
  6.5 54.8 %all-reduce.11.cloned.1.call-start = ((), (), s32[]{:S(2)}) async-start(), calls=%async_computation.4 | async-start | bytes 393216 | tf_op jit(solution)/shard_map/psum | solution.py:21
  10.4 98.9 %all-reduce.9.cloned.1.call-start = ((), (), s32[]{:S(2)}) async-start(), calls=%async_computation.3 | async-start | bytes 393216 | tf_op jit(solution)/shard_map/psum | solution.py:21
  61.4 255.5 %all-reduce.7.cloned.1.call-start = ((), (), s32[]{:S(2)}) async-start(), calls=%async_computation.2 | async-start | bytes 1179648 | tf_op jit(solution)/shard_map/psum | solution.py:26
  138.5 332.9 %all-gather.2.cloned.1.call-start = ((), (), s32[]{:S(2)}) async-start(), calls=%async_computation.1 | async-start | bytes 8912896 | tf_op jit(solution)/shard_map/all_gather | solution.py:36
Sparse Core Ops, SparseCore 0:
  10.5 50.8 all-reduce.10
  63.8 45.3 all-reduce.8
  138.6 178.1 all-reduce.6
  366.8 104.6 all-gather.1
